TPU v7x, 32 devices: a whole 2x2x4 slice. The times are simulated.
32 devices in a mesh: dp: 8 (over z, core), fsdp: 4 (over y, x).
Axes of the slice: x: 2, y: 2, z: 4, core: 2. Of those that a mesh axis runs over, the one named last changes fastest.
Arguments:
- pixels: bfloat16 [32768, 768], P(('dp', 'fsdp')), may hold values from -6 to 6
- valid_mask: int32 [32768, 768], P(('dp', 'fsdp')), may hold values from 0 to 1
- size_groups: int32 [32], P(('dp', 'fsdp')), may hold values from 0 to 2
- code_index: int32 [4, 8192], P(None, ('dp', 'fsdp')), may hold values from 0 to 16383, as said below
- w_pixel: float32 [2, 768, 512], P(None, 'fsdp', 'dp'), may hold values from -0.625 to 0.625
- w_res: float32 [4, 4608, 512], P(None, 'fsdp', 'dp'), may hold values from -0.1875 to 0.1875
- w_scale: float32 [2, 2048, 512], P(None, 'fsdp', 'dp'), may hold values from -0.5 to 0.5
- w_latent: float32 [2, 512, 256], P(None, 'fsdp', 'dp'), may hold values from -0.75 to 0.75
- norm_gains: float32 [8, 512], replicated, may hold values from -0.9 to 1.5
- moment_pixel: float32 [2, 768, 512], P(None, 'fsdp', 'dp'), may hold values from -4.4703484e-08 to 4.4703484e-08
- moment_res: float32 [4, 4608, 512], P(None, 'fsdp', 'dp'), may hold values from -4.4703484e-08 to 4.4703484e-08
- moment_scale: float32 [2, 2048, 512], P(None, 'fsdp', 'dp'), may hold values from -4.4703484e-08 to 4.4703484e-08
- moment_latent: float32 [2, 512, 256], P(None, 'fsdp', 'dp'), may hold values from -4.4703484e-08 to 4.4703484e-08
- moment_gains: float32 [8, 512], replicated, may hold values from -1.4901161e-07 to 1.4901161e-07
- second_pixel: float32 [2, 768, 512], P(None, 'fsdp', 'dp'), may hold values from 7.84e-18 to 3.136e-17
- second_res: float32 [4, 4608, 512], P(None, 'fsdp', 'dp'), may hold values from 7.84e-18 to 3.136e-17
- second_scale: float32 [2, 2048, 512], P(None, 'fsdp', 'dp'), may hold values from 7.84e-18 to 3.136e-17
- second_latent: float32 [2, 512, 256], P(None, 'fsdp', 'dp'), may hold values from 7.84e-18 to 3.136e-17
- second_gains: float32 [8, 512], replicated, may hold values from 1e-16 to 4e-16
- ema_counts: float32 [16384], P(('dp', 'fsdp')), may hold values from 0.5 to 4
- ema_sums: float32 [16384, 256], P(('dp', 'fsdp')), may hold values from -6 to 6
Outputs:
- loss_parts: float32 [3], replicated
- grad_norm: float32 [1], replicated
- next_pixel: float32 [2, 768, 512], P(None, 'fsdp', 'dp')
- next_moment_pixel: float32 [2, 768, 512], P(None, 'fsdp', 'dp')
- next_second_pixel: float32 [2, 768, 512], P(None, 'fsdp', 'dp')
- copy_pixel: bfloat16 [2, 768, 512], P(None, 'fsdp', 'dp')
- next_res: float32 [4, 4608, 512], P(None, 'fsdp', 'dp')
- next_moment_res: float32 [4, 4608, 512], P(None, 'fsdp', 'dp')
- next_second_res: float32 [4, 4608, 512], P(None, 'fsdp', 'dp')
- copy_res: bfloat16 [4, 4608, 512], P(None, 'fsdp', 'dp')
- next_scale: float32 [2, 2048, 512], P(None, 'fsdp', 'dp')
- next_moment_scale: float32 [2, 2048, 512], P(None, 'fsdp', 'dp')
- next_second_scale: float32 [2, 2048, 512], P(None, 'fsdp', 'dp')
- copy_scale: bfloat16 [2, 2048, 512], P(None, 'fsdp', 'dp')
- next_latent: float32 [2, 512, 256], P(None, 'fsdp', 'dp')
- next_moment_latent: float32 [2, 512, 256], P(None, 'fsdp', 'dp')
- next_second_latent: float32 [2, 512, 256], P(None, 'fsdp', 'dp')
- copy_latent: bfloat16 [2, 512, 256], P(None, 'fsdp', 'dp')
- next_gains: float32 [8, 512], replicated
- next_moment_gains: float32 [8, 512], replicated
- next_second_gains: float32 [8, 512], replicated
- next_counts: float32 [16384], P(('dp', 'fsdp'))
- next_sums: float32 [16384, 256], P(('dp', 'fsdp'))
- codebook: float32 [16384, 256], P(('dp', 'fsdp'))
- codebook_copy: bfloat16 [16384, 256], P(('dp', 'fsdp'))
Inputs may be any that keep to these rules, and one draw needn't show every extreme that they name: `code_index`: among the 4 x 256 codes of one device's positions, at most 64 lie in any one device's block of 16384 / 32 consecutive codes, and on every device some block holds exactly 64 of them.
All inputs are finite; a program needn't handle non-finite values.
Results may differ from a plain program's by a relative error of at most 0.0061.
Values may be sent and summed in bfloat16 or wider, within the bound.
No kernel may reach another device: no remote copies, remote signals or barrier semaphores. Data moves between devices by JAX's collectives and lax.ppermute only.
A program may use at most 256 MiB of HBM per device.

v0:
```python
import jax
import jax.numpy as jnp
from jax import lax
from jax.sharding import PartitionSpec as P

C = 512
ZD = 256
K = 16384
GROUPS = 32
SIDE = 32
DEPTH = 4
STEP = 5
HIGH = lax.Precision.HIGHEST
TAPS = [(dy, dx) for dy in (-1, 0, 1) for dx in (-1, 0, 1)]
COMMIT_WEIGHT = 0.25
CLIP_AT = 1e-05
EMA_DECAY = 0.8
WEIGHT_RATE = 0.03
GAIN_RATE = 0.4


def geometry(groups, size, width):
    span = jnp.left_shift(jnp.ones_like(groups), groups)
    sides = size // 4 * span
    tile = jnp.arange(16, dtype=jnp.int32)[None, :]
    image = tile // 4 // span[:, None] * (4 // span[:, None]) + tile % 4 // span[:, None]
    member = (image[:, :, None] == jnp.arange(16, dtype=jnp.int32)[None, None, :]).astype(
        jnp.float32
    )
    count = (sides * sides).astype(jnp.float32) * (width // GROUPS)
    return (sides, member, count)


def image_means(field, member, count):
    batch, size, _, width = field.shape
    tile = size // 4
    sums = jnp.sum(field.reshape(batch, 4, tile, 4, tile, width), axis=(2, 4)).reshape(
        batch, 16, width
    )
    per_image = jnp.einsum("btm,btc->bmc", member, sums, precision=HIGH)
    grouped = (
        jnp.sum(per_image.reshape(batch, 16, GROUPS, width // GROUPS), axis=3)
        / count[:, None, None]
    )
    spread = jnp.einsum("btm,bmg->btg", member, grouped, precision=HIGH)
    full = jnp.repeat(spread, width // GROUPS, axis=2).reshape(batch, 4, 1, 4, 1, width)
    return jnp.broadcast_to(full, (batch, 4, tile, 4, tile, width)).reshape(
        batch, size, size, width
    )


def gn_silu(field, gamma, beta, geom):
    mean = image_means(field, geom[1], geom[2])
    centered = field - mean
    var = image_means(centered * centered, geom[1], geom[2])
    return jax.nn.silu(centered * lax.rsqrt(var + 1e-05) * gamma + beta)


def silu_slope(value):
    gate = jax.nn.sigmoid(value)
    return gate * (1.0 + value * (1.0 - gate))


def side_masks(sides, size, delta):
    pos = jnp.arange(size, dtype=jnp.int32)
    near = pos + delta
    inside = (near >= 0) & (near < size)
    same = near[None, :] // sides[:, None] == pos[None, :] // sides[:, None]
    return (inside[None, :] & same).astype(jnp.float32)


def shifted(act, sides, dy, dx):
    size = act.shape[1]
    padded = jnp.pad(act, ((0, 0), (1, 1), (1, 1), (0, 0)))
    part = padded[:, 1 + dy : 1 + dy + size, 1 + dx : 1 + dx + size, :]
    keep = side_masks(sides, size, dy)[:, :, None] * side_masks(sides, size, dx)[:, None, :]
    return part * keep[..., None].astype(act.dtype)


def along_rows(left, right):
    return lax.dot_general(
        left, right, (((0,), (0,)), ((), ())), preferred_element_type=jnp.float32
    )


def along_cols(left, right):
    return lax.dot_general(
        left, right, (((1,), (1,)), ((), ())), preferred_element_type=jnp.float32
    )


def conv_forward(act, taps, geom):
    width = act.shape[3]
    total = jnp.zeros((act.shape[0] * act.shape[1] * act.shape[2], width), jnp.float32)
    for index, (dy, dx) in enumerate(TAPS):
        piece = shifted(act, geom[0], dy, dx).reshape(-1, width)
        total = total + jnp.dot(piece, taps[index], preferred_element_type=jnp.float32)
    return total.reshape(act.shape)


def conv_backward(act, taps, grad_out, geom):
    width = act.shape[3]
    grad_low = grad_out.reshape(-1, width).astype(jnp.bfloat16)
    weight_parts = []
    grad_act = jnp.zeros(act.shape, jnp.float32)
    for index, (dy, dx) in enumerate(TAPS):
        piece = shifted(act, geom[0], dy, dx).reshape(-1, width)
        weight_parts.append(along_rows(piece, grad_low))
        back = along_cols(grad_low, taps[index]).reshape(act.shape)
        grad_act = grad_act + shifted(back, geom[0], -dy, -dx)
    return (jnp.concatenate(weight_parts, axis=0), grad_act)


def block_forward(field, taps_pair, gains, first, geom):
    a_one = gn_silu(field, gains[first], gains[4 + first], geom).astype(jnp.bfloat16)
    t_one = conv_forward(a_one, taps_pair[0], geom)
    a_two = gn_silu(t_one, gains[first + 1], gains[5 + first], geom).astype(jnp.bfloat16)
    t_two = conv_forward(a_two, taps_pair[1], geom)
    return (field + t_two, (field, a_one, t_one, a_two))


def block_backward(grad, kept, taps_pair, gains, first, geom):
    field, a_one, t_one, a_two = kept
    grad_two, d_a_two = conv_backward(a_two, taps_pair[1], grad, geom)
    _, pull = jax.vjp(
        lambda x, g, b: gn_silu(x, g, b, geom), t_one, gains[first + 1], gains[5 + first]
    )
    d_t_one, scale_two, shift_two = pull(d_a_two)
    grad_one, d_a_one = conv_backward(a_one, taps_pair[0], d_t_one, geom)
    _, pull = jax.vjp(lambda x, g, b: gn_silu(x, g, b, geom), field, gains[first], gains[4 + first])
    d_field, scale_one, shift_one = pull(d_a_one)
    return (grad + d_field, (grad_one, grad_two), (scale_one, scale_two, shift_one, shift_two))


def to_depth(field):
    batch, size, _, width = field.shape
    half = size // 2
    parts = field.reshape(batch, half, 2, half, 2, width).transpose(0, 1, 3, 2, 4, 5)
    return parts.reshape(batch * half * half, 4 * width)


def from_depth(rows, batch, size):
    half = size // 2
    width = rows.shape[1] // 4
    parts = rows.reshape(batch, half, half, 2, 2, width).transpose(0, 1, 3, 2, 4, 5)
    return parts.reshape(batch, size, size, width)


def fetch(shard):
    cols = lax.all_gather(shard.astype(jnp.bfloat16), "dp", axis=1, tiled=True)
    return lax.all_gather(cols, "fsdp", axis=0, tiled=True)


def backward_copy(shard, ready):
    return fetch(shard).reshape(ready.shape)


def reduce_grad(full):
    rows = lax.psum_scatter(full, "fsdp", scatter_dimension=0, tiled=True)
    return lax.psum_scatter(rows, "dp", scatter_dimension=1, tiled=True)


def adam_step(weight, moment, second, grad, rate):
    moment_new = 0.5 * moment + 0.5 * grad
    second_new = 0.5 * second + 0.5 * grad * grad
    fix = 1.0 - 0.5**STEP
    weight_new = weight - rate * (
        moment_new / fix / (jnp.sqrt(second_new / fix) + 1e-12) + 0.01 * weight
    )
    return (weight_new, moment_new, second_new)


def owner_slots(flat_codes, devices, capacity, rows_own):
    owner = flat_codes // rows_own
    order = jnp.argsort(owner, stable=True)
    ranked = owner[order]
    first = jnp.searchsorted(ranked, jnp.arange(devices, dtype=jnp.int32))
    place = jnp.arange(flat_codes.shape[0], dtype=jnp.int32) - first[ranked]
    return jnp.zeros_like(flat_codes).at[order].set(ranked * capacity + place)


def on_device(
    pixels,
    valid_mask,
    size_groups,
    code_index,
    w_pixel,
    w_res,
    w_scale,
    w_latent,
    norm_gains,
    moment_pixel,
    moment_res,
    moment_scale,
    moment_latent,
    moment_gains,
    second_pixel,
    second_res,
    second_scale,
    second_latent,
    second_gains,
    ema_counts,
    ema_sums,
):
    canv = size_groups.shape[0]
    n_outer = lax.axis_size("dp")
    n_inner = lax.axis_size("fsdp")
    devices = n_outer * n_inner
    latent_all = code_index.shape[1] * devices
    rows = ema_sums.shape[0]
    flat_codes = code_index.reshape(-1)
    capacity = max(2, 2 * flat_codes.shape[0] // devices)
    slot = owner_slots(flat_codes, devices, capacity, rows)
    local_row = flat_codes % rows
    geom = geometry(size_groups, SIDE, C)
    mask = valid_mask.astype(jnp.float32)
    total_valid = lax.psum(jnp.sum(mask), ("dp", "fsdp"))
    book = (ema_sums / ema_counts[:, None]).astype(jnp.bfloat16)
    wanted = jnp.full((devices * capacity,), -1, jnp.int32).at[slot].set(local_row)
    wanted = wanted.reshape(n_outer, n_inner, capacity)
    asked = lax.all_to_all(
        lax.all_to_all(wanted, "dp", split_axis=0, concat_axis=0, tiled=True),
        "fsdp",
        split_axis=1,
        concat_axis=1,
        tiled=True,
    )
    answer = jnp.take(book, jnp.maximum(asked, 0), axis=0)
    replies = lax.all_to_all(
        lax.all_to_all(answer, "dp", split_axis=0, concat_axis=0, tiled=True),
        "fsdp",
        split_axis=1,
        concat_axis=1,
        tiled=True,
    )
    picked_rows = replies.reshape(devices * capacity, -1)[slot].reshape(
        code_index.shape + (book.shape[1],)
    )
    q_cum = jnp.cumsum(picked_rows.astype(jnp.float32), axis=0)
    patch_in = fetch(w_pixel[0])
    field = jnp.dot(pixels, patch_in, preferred_element_type=jnp.float32).reshape(
        canv, SIDE, SIDE, C
    )
    enc_taps = (fetch(w_res[0]).reshape(9, C, C), fetch(w_res[1]).reshape(9, C, C))
    field, kept_enc = block_forward(field, enc_taps, norm_gains, 0, geom)
    e_four = to_depth(field.astype(jnp.bfloat16))
    w_down = fetch(w_scale[0])
    hidden = jnp.dot(e_four, w_down, preferred_element_type=jnp.float32)
    s_one = jax.nn.silu(hidden).astype(jnp.bfloat16)
    w_proj = fetch(w_latent[0])
    latent = jnp.dot(s_one, w_proj, preferred_element_type=jnp.float32)
    diff = latent[None] - q_cum
    commit = jnp.sum(diff * diff)
    shift = q_cum[DEPTH - 1] - latent
    quant = (latent + shift).astype(jnp.bfloat16)
    w_back = fetch(w_latent[1])
    inner = along_cols(quant, w_back)
    s_two = jax.nn.silu(inner).astype(jnp.bfloat16)
    w_up = fetch(w_scale[1])
    upper = along_cols(s_two, w_up)
    dec_field = from_depth(upper, canv, SIDE)
    dec_taps = (fetch(w_res[2]).reshape(9, C, C), fetch(w_res[3]).reshape(9, C, C))
    dec_field, kept_dec = block_forward(dec_field, dec_taps, norm_gains, 2, geom)
    outer = jax.nn.silu(dec_field).astype(jnp.bfloat16).reshape(-1, C)
    w_head = fetch(w_pixel[1])
    recon = along_cols(outer, w_head)
    err = recon - pixels.astype(jnp.float32)
    smooth = jnp.sqrt(err * err + 1.0)
    l1_local = jnp.sum(mask * (smooth - 1.0))
    grad_rec = (mask * err / smooth / total_valid).astype(jnp.bfloat16)
    d_head = along_rows(grad_rec, outer)
    head_b = backward_copy(w_pixel[1], w_head)
    d_outer = jnp.dot(grad_rec, head_b, preferred_element_type=jnp.float32)
    d_dec = (d_outer * silu_slope(dec_field.reshape(-1, C))).reshape(dec_field.shape)
    dec_b = (backward_copy(w_res[2], dec_taps[0]), backward_copy(w_res[3], dec_taps[1]))
    d_dec, dec_grads, dec_gain = block_backward(d_dec, kept_dec, dec_b, norm_gains, 2, geom)
    d_upper = to_depth(d_dec).astype(jnp.bfloat16)
    d_up = along_rows(d_upper, s_two)
    up_b = backward_copy(w_scale[1], w_up)
    d_s_two = jnp.dot(d_upper, up_b, preferred_element_type=jnp.float32)
    d_inner = (d_s_two * silu_slope(inner)).astype(jnp.bfloat16)
    d_back = along_rows(d_inner, quant)
    back_b = backward_copy(w_latent[1], w_back)
    d_quant = jnp.dot(d_inner, back_b, preferred_element_type=jnp.float32)
    d_latent = d_quant + 2.0 * COMMIT_WEIGHT / (latent_all * ZD) * jnp.sum(diff, axis=0)
    d_latent = d_latent.astype(jnp.bfloat16)
    d_proj = along_rows(s_one, d_latent)
    proj_b = backward_copy(w_latent[0], w_proj)
    d_s_one = along_cols(d_latent, proj_b)
    d_hidden = (d_s_one * silu_slope(hidden)).astype(jnp.bfloat16)
    d_down = along_rows(e_four, d_hidden)
    down_b = backward_copy(w_scale[0], w_down)
    d_e_four = along_cols(d_hidden, down_b)
    d_enc = from_depth(d_e_four, canv, SIDE)
    enc_b = (backward_copy(w_res[0], enc_taps[0]), backward_copy(w_res[1], enc_taps[1]))
    d_enc, enc_grads, enc_gain = block_backward(d_enc, kept_enc, enc_b, norm_gains, 0, geom)
    d_first = d_enc.reshape(-1, C).astype(jnp.bfloat16)
    d_patch = along_rows(pixels, d_first)
    grad_pixel = jnp.stack([reduce_grad(d_patch), reduce_grad(d_head)])
    grad_res = jnp.stack(
        [
            reduce_grad(enc_grads[0]),
            reduce_grad(enc_grads[1]),
            reduce_grad(dec_grads[0]),
            reduce_grad(dec_grads[1]),
        ]
    )
    grad_scale = jnp.stack([reduce_grad(d_down), reduce_grad(d_up)])
    grad_latent = jnp.stack([reduce_grad(d_proj), reduce_grad(d_back)])
    gain_local = jnp.stack(
        [
            enc_gain[0],
            enc_gain[1],
            dec_gain[0],
            dec_gain[1],
            enc_gain[2],
            enc_gain[3],
            dec_gain[2],
            dec_gain[3],
        ]
    )
    grad_gains, smooth_sum, commit_sum = lax.psum((gain_local, l1_local, commit), ("dp", "fsdp"))
    shard_squares = jnp.sum(grad_pixel * grad_pixel) + jnp.sum(grad_res * grad_res)
    shard_squares = (
        shard_squares + jnp.sum(grad_scale * grad_scale) + jnp.sum(grad_latent * grad_latent)
    )
    total_squares = lax.psum(shard_squares, ("dp", "fsdp")) + jnp.sum(grad_gains * grad_gains)
    norm = jnp.sqrt(total_squares)
    factor = CLIP_AT / jnp.maximum(norm, CLIP_AT)
    groups_all = [
        (w_pixel, moment_pixel, second_pixel, grad_pixel),
        (w_res, moment_res, second_res, grad_res),
        (w_scale, moment_scale, second_scale, grad_scale),
        (w_latent, moment_latent, second_latent, grad_latent),
    ]
    outputs = [jnp.stack([smooth_sum, total_valid, commit_sum]), norm.reshape(1)]
    for weight, moment, second, grad in groups_all:
        weight_new, moment_new, second_new = adam_step(
            weight, moment, second, grad * factor, WEIGHT_RATE
        )
        outputs += [weight_new, moment_new, second_new, weight_new.astype(jnp.bfloat16)]
    outputs += list(
        adam_step(norm_gains, moment_gains, second_gains, grad_gains * factor, GAIN_RATE)
    )
    prev = jnp.concatenate([jnp.zeros_like(q_cum[:1]), q_cum[:-1]], axis=0)
    resid = (latent[None] - prev).astype(jnp.bfloat16).reshape(-1, ZD)
    block_len = min(K, 2048)

    def code_block(start):
        onehot = (
            flat_codes[:, None] == start + jnp.arange(block_len, dtype=jnp.int32)[None, :]
        ).astype(jnp.bfloat16)
        return (along_rows(onehot, resid), jnp.sum(onehot, axis=0, dtype=jnp.float32))

    sums_all, counts_all = lax.map(code_block, jnp.arange(0, K, block_len, dtype=jnp.int32))
    sums_all = sums_all.reshape(K, ZD)
    counts_all = counts_all.reshape(K)
    sums_total, counts_total = lax.psum((sums_all, counts_all), ("dp", "fsdp"))
    start_row = lax.axis_index(("dp", "fsdp")) * rows
    my_sums = lax.dynamic_slice_in_dim(sums_total, start_row, rows, 0)
    my_counts = lax.dynamic_slice_in_dim(counts_total, start_row, rows, 0)
    counts_new = EMA_DECAY * ema_counts + (1.0 - EMA_DECAY) * my_counts
    sums_new = EMA_DECAY * ema_sums + (1.0 - EMA_DECAY) * my_sums
    book_new = sums_new / counts_new[:, None]
    outputs += [counts_new, sums_new, book_new, book_new.astype(jnp.bfloat16)]
    return tuple(outputs)


def solution(mesh):
    placed = (
        P(("dp", "fsdp"), None),
        P(("dp", "fsdp"), None),
        P(("dp", "fsdp")),
        P(None, ("dp", "fsdp")),
        P(None, "fsdp", "dp"),
        P(None, "fsdp", "dp"),
        P(None, "fsdp", "dp"),
        P(None, "fsdp", "dp"),
        P(),
        P(None, "fsdp", "dp"),
        P(None, "fsdp", "dp"),
        P(None, "fsdp", "dp"),
        P(None, "fsdp", "dp"),
        P(),
        P(None, "fsdp", "dp"),
        P(None, "fsdp", "dp"),
        P(None, "fsdp", "dp"),
        P(None, "fsdp", "dp"),
        P(),
        P(("dp", "fsdp")),
        P(("dp", "fsdp"), None),
    )
    return jax.shard_map(
        on_device,
        mesh=mesh,
        in_specs=placed,
        out_specs=(
            P(),
            P(),
            P(None, "fsdp", "dp"),
            P(None, "fsdp", "dp"),
            P(None, "fsdp", "dp"),
            P(None, "fsdp", "dp"),
            P(None, "fsdp", "dp"),
            P(None, "fsdp", "dp"),
            P(None, "fsdp", "dp"),
            P(None, "fsdp", "dp"),
            P(None, "fsdp", "dp"),
            P(None, "fsdp", "dp"),
            P(None, "fsdp", "dp"),
            P(None, "fsdp", "dp"),
            P(None, "fsdp", "dp"),
            P(None, "fsdp", "dp"),
            P(None, "fsdp", "dp"),
            P(None, "fsdp", "dp"),
            P(),
            P(),
            P(),
            P(("dp", "fsdp")),
            P(("dp", "fsdp"), None),
            P(("dp", "fsdp"), None),
            P(("dp", "fsdp"), None),
        ),
        check_vma=False,
    )
```

profile of v0, /device:TPU:12, one launch (start us, length us, event | category | flops | bytes accessed | tf_op | source)
XLA Modules:
  0.0 1944.9 jit_solution(17899605121491176382)
XLA Ops:
  11.5 22.5 %all-gather.31.cloned.1.call-done = bf16[1,1152,512]{1,2,0:T(8,128)(2,1)} async-done(((bf16[1,1152,64]{1,2,0:T(8,128)(2,1)}), bf16[1,1152,512]{1,2,0:T(8,128)(2,1)}) %all-gather.31.cloned.1.call-update) | async-done | bytes 1179664 | tf_op jit(solution)/shard_map/all_gather | solution.py:150
  36.5 22.2 %all-gather.35.cloned.1.call-done = bf16[1,1152,512]{1,2,0:T(8,128)(2,1)} async-done(((bf16[1,1152,64]{1,2,0:T(8,128)(2,1)}), bf16[1,1152,512]{1,2,0:T(8,128)(2,1)}) %all-gather.35.cloned.1.call-update) | async-done | bytes 1179664 | tf_op jit(solution)/shard_map/all_gather | solution.py:150
  61.2 15.9 all-gather.6
  77.2 16.3 all-gather.12
  119.3 15.9 fusion.437
  208.5 29.5 %all-gather.10 = bf16[1,128,256]{1,2,0:T(8,128)(2,1)S(1)} all-gather(bf16[1,128,32]{1,2,0:T(8,128)(2,1)S(1)} %get-tuple-element.455), channel_id=12, replica_groups=mesh['dp'=8,'fsdp'=4] {'dp'}, dimensions={2}, use_global_device_ids=true | all-gather | bytes 73728 | tf_op jit(solution)/shard_map/all_gather | solution.py:150
  471.4 41.4 %psum.50 = f32[]{:T(128)} all-reduce(f32[]{:T(128)} %get-tuple-element.298), channel_id=1, replica_groups=mesh['dp'=8,'fsdp'=4] {'dp','fsdp'}, use_global_device_ids=true, to_apply=%region_27.30 | all-reduce | flops 1 | bytes 8 | tf_op jit(solution)/shard_map/psum | solution.py:217
  795.2 49.7 %while.36 = (s32[]{:T(128)}, f32[8,2048,256]{2,1,0:T(8,128)}, f32[8,2048]{1,0:T(8,128)S(1)}, s32[4,256]{1,0:T(4,128)S(1)}, s32[8]{0:T(128)S(1)}, /*index=5*/bf16[1024,256]{1,0:T(8,128)(2,1)S(1)}, s32[]{:T(128)}, s32[]{:T(128)}) while((s32[]{:T(128)}, f32[8,2048,256]{2,1,0:T(8,128)}, f32[8,2048]{1,0:T(8,128)S(1)}, s32[4,256]{1,0:T(4,128)S(1)}, ...), condition=%wide.region_84.87_spmd, body=%wide.region_82.86_spmd.sunk | while | flops 1084227584 | bytes 2687093 | solution.py:355
  851.7 95.4 %reduce-scatter.45.cloned.1.call-done = f32[1152,512]{1,0:T(8,128)} async-done(((f32[4608,512]{1,0:T(8,128)}), f32[1152,512]{1,0:T(8,128)}) %reduce-scatter.45.cloned.1.call-update) | async-done | bytes 2359312 | tf_op jit(solution)/shard_map/reduce_scatter | solution.py:159
  950.2 94.9 %reduce-scatter.47.cloned.1.call-done = f32[1152,512]{1,0:T(8,128)} async-done(((f32[4608,512]{1,0:T(8,128)}), f32[1152,512]{1,0:T(8,128)}) %reduce-scatter.47.cloned.1.call-update) | async-done | bytes 2359312 | tf_op jit(solution)/shard_map/reduce_scatter | solution.py:159
  1048.3 95.0 %reduce-scatter.49.cloned.1.call-done = f32[1152,512]{1,0:T(8,128)} async-done(((f32[4608,512]{1,0:T(8,128)}), f32[1152,512]{1,0:T(8,128)}) %reduce-scatter.49.cloned.1.call-update) | async-done | bytes 2359312 | tf_op jit(solution)/shard_map/reduce_scatter | solution.py:159
  1146.4 94.9 %reduce-scatter.51.cloned.1.call-done = f32[1152,512]{1,0:T(8,128)} async-done(((f32[4608,512]{1,0:T(8,128)}), f32[1152,512]{1,0:T(8,128)}) %reduce-scatter.51.cloned.1.call-update) | async-done | bytes 2359312 | tf_op jit(solution)/shard_map/reduce_scatter | solution.py:159
  1245.8 25.0 %reduce-scatter.77.cloned.1.call-done = f32[32,128]{1,0:T(8,128)} async-done(((f32[256,128]{1,0:T(8,128)}), f32[32,128]{1,0:T(8,128)}) %reduce-scatter.77.cloned.1.call-update) | async-done | bytes 16400
  1271.7 30.3 %reduce-scatter.79.cloned.1.call-done = f32[32,128]{1,0:T(8,128)} async-done(((f32[256,128]{1,0:T(8,128)}), f32[32,128]{1,0:T(8,128)}) %reduce-scatter.79.cloned.1.call-update) | async-done | bytes 16400
  1303.5 30.4 %reduce-scatter.43.cloned.1.call-done = f32[192,64]{0,1:T(8,128)} async-done(((f32[192,512]{0,1:T(8,128)}), f32[192,64]{0,1:T(8,128)}) %reduce-scatter.43.cloned.1.call-update) | async-done | bytes 49168 | tf_op jit(solution)/shard_map/reduce_scatter | solution.py:160
  1334.0 31.9 %reduce-scatter.41.cloned.1.call-done = f32[192,64]{0,1:T(8,128)} async-done(((f32[192,512]{0,1:T(8,128)}), f32[192,64]{0,1:T(8,128)}) %reduce-scatter.41.cloned.1.call-update) | async-done | bytes 49168 | tf_op jit(solution)/shard_map/reduce_scatter | solution.py:160
  1367.4 288.5 %all-reduce.41.cloned.1.call-done = (f32[16384]{0:T(1024)}, f32[16384,256]{1,0:T(8,128)}) async-done(((f32[16384]{0:T(1024)}, f32[16384,256]{1,0:T(8,128)}), (f32[16384]{0:T(1024)}, f32[16384,256]{1,0:T(8,128)})) %all-reduce.41.cloned.1.call-update) | async-done | bytes 16842768 | tf_op jit(solution)/shard_map/psum | solution.py:358
  1658.8 28.4 %reduce-scatter.75.cloned.1.call-done = f32[64,512]{1,0:T(8,128)} async-done(((f32[512,512]{1,0:T(8,128)}), f32[64,512]{1,0:T(8,128)}) %reduce-scatter.75.cloned.1.call-update) | async-done | bytes 131088
  1687.2 33.6 %reduce-scatter.73.cloned.1.call-done = f32[64,512]{1,0:T(8,128)} async-done(((f32[512,512]{1,0:T(8,128)}), f32[64,512]{1,0:T(8,128)}) %reduce-scatter.73.cloned.1.call-update) | async-done | bytes 131088
  1722.4 35.2 %reduce-scatter.65.cloned.1.call-done = f32[64,1152]{1,0:T(8,128)} async-done(((f32[512,1152]{1,0:T(8,128)}), f32[64,1152]{1,0:T(8,128)}) %reduce-scatter.65.cloned.1.call-update) | async-done | bytes 294928
  1757.6 37.8 %reduce-scatter.67.cloned.1.call-done = f32[64,1152]{1,0:T(8,128)} async-done(((f32[512,1152]{1,0:T(8,128)}), f32[64,1152]{1,0:T(8,128)}) %reduce-scatter.67.cloned.1.call-update) | async-done | bytes 294928
  1795.4 37.7 %reduce-scatter.69.cloned.1.call-done = f32[64,1152]{1,0:T(8,128)} async-done(((f32[512,1152]{1,0:T(8,128)}), f32[64,1152]{1,0:T(8,128)}) %reduce-scatter.69.cloned.1.call-update) | async-done | bytes 294928
  1833.0 37.8 %reduce-scatter.71.cloned.1.call-done = f32[64,1152]{1,0:T(8,128)} async-done(((f32[512,1152]{1,0:T(8,128)}), f32[64,1152]{1,0:T(8,128)}) %reduce-scatter.71.cloned.1.call-update) | async-done | bytes 294928
  1875.8 44.7 %all-reduce.37 = (f32[1]{0:T(128)}, f32[1]{0:T(128)}, f32[]{:T(128)}, f32[8,512]{1,0:T(8,128)}) all-reduce(f32[1]{0:T(128)} %bitcast.179, f32[1]{0:T(128)} %bitcast.177, f32[]{:T(128)S(6)} %add.1351, f32[8,512]{1,0:T(8,128)} %stack.107), channel_id=1, replica_groups=mesh['dp'=8,'fsdp'=4] {'dp','fsdp'}, use_global_device_ids=true, to_apply=%region_29.32 | all-reduce | flops 4099 | bytes 32792 | tf_op jit(solution)/shard_map/psum | solution.py:322
  (1059 shorter events, 722.9 us)
Async XLA Ops:
  10.9 314.8 %all-gather.47.cloned.1.call-start = ((), (), s32[]{:S(2)}) async-start(), calls=%async_computation.42 | async-start | bytes 1327104 | tf_op jit(solution)/shard_map/all_gather | solution.py:150
  11.5 322.0 %all-gather.33.cloned.1.call-start = ((), (), s32[]{:S(2)}) async-start(), calls=%async_computation.35 | async-start | bytes 5898240 | tf_op jit(solution)/shard_map/all_gather | solution.py:151
  36.4 333.2 %all-gather.37.cloned.1.call-start = ((), (), s32[]{:S(2)}) async-start(), calls=%async_computation.37 | async-start | bytes 5898240 | tf_op jit(solution)/shard_map/all_gather | solution.py:151
  61.1 323.2 %all-gather.39.cloned.1.call-start = ((), (), s32[]{:S(2)}) async-start(), calls=%async_computation.38 | async-start | bytes 2621440 | tf_op jit(solution)/shard_map/all_gather | solution.py:151
  77.2 311.2 %all-gather.41.cloned.1.call-start = ((), (), s32[]{:S(2)}) async-start(), calls=%async_computation.39 | async-start | bytes 2621440 | tf_op jit(solution)/shard_map/all_gather | solution.py:151
  93.5 331.1 %all-gather.45.cloned.1.call-start = ((), (), s32[]{:S(2)}) async-start(), calls=%async_computation.41 | async-start | bytes 5898240 | tf_op jit(solution)/shard_map/all_gather | solution.py:151
  266.1 184.8 %all-gather.49.cloned.1.call-start = ((), (), s32[]{:S(2)}) async-start(), calls=%async_computation.43 | async-start | bytes 5898240 | tf_op jit(solution)/shard_map/all_gather | solution.py:151
  325.8 461.3 %reduce-scatter.57.cloned.1.call-start = ((), (), s32[]{:S(2)}) async-start(), calls=%async_computation.32 | async-start | bytes 655360 | tf_op jit(solution)/shard_map/reduce_scatter | solution.py:159
  607.9 181.0 %reduce-scatter.59.cloned.1.call-start = ((), (), s32[]{:S(2)}) async-start(), calls=%async_computation.33 | async-start | bytes 655360 | tf_op jit(solution)/shard_map/reduce_scatter | solution.py:159
  714.1 233.0 %reduce-scatter.45.cloned.1.call-start = ((), (), s32[]{:S(2)}) async-start(), calls=%async_computation.26 | async-start | bytes 11796480 | tf_op jit(solution)/shard_map/reduce_scatter | solution.py:159
  730.8 314.3 %reduce-scatter.47.cloned.1.call-start = ((), (), s32[]{:S(2)}) async-start(), calls=%async_computation.27 | async-start | bytes 11796480 | tf_op jit(solution)/shard_map/reduce_scatter | solution.py:159
  748.0 395.2 %reduce-scatter.49.cloned.1.call-start = ((), (), s32[]{:S(2)}) async-start(), calls=%async_computation.28 | async-start | bytes 11796480 | tf_op jit(solution)/shard_map/reduce_scatter | solution.py:159
  769.9 471.4 %reduce-scatter.51.cloned.1.call-start = ((), (), s32[]{:S(2)}) async-start(), calls=%async_computation.29 | async-start | bytes 11796480 | tf_op jit(solution)/shard_map/reduce_scatter | solution.py:159
  787.0 483.9 %reduce-scatter.77.cloned.1.call-start = ((), (), s32[]{:S(2)}) async-start(), calls=%async_computation.52 | async-start | bytes 147456
  788.8 513.2 %reduce-scatter.79.cloned.1.call-start = ((), (), s32[]{:S(2)}) async-start(), calls=%async_computation.53 | async-start | bytes 147456
  790.6 543.4 %reduce-scatter.43.cloned.1.call-start = ((), (), s32[]{:S(2)}) async-start(), calls=%async_computation.25 | async-start | bytes 589824 | tf_op jit(solution)/shard_map/reduce_scatter | solution.py:160
  792.7 573.2 %reduce-scatter.41.cloned.1.call-start = ((), (), s32[]{:S(2)}) async-start(), calls=%async_computation.24 | async-start | bytes 589824 | tf_op jit(solution)/shard_map/reduce_scatter | solution.py:160
  794.8 861.0 %all-reduce.41.cloned.1.call-start = ((), (), s32[]{:S(2)}) async-start(), calls=%async_computation.54 | async-start | bytes 33685504 | tf_op jit(solution)/shard_map/psum | solution.py:358
  845.6 841.6 %reduce-scatter.75.cloned.1.call-start = ((), (), s32[]{:S(2)}) async-start(), calls=%async_computation.51 | async-start | bytes 1179648
  848.2 872.5 %reduce-scatter.73.cloned.1.call-start = ((), (), s32[]{:S(2)}) async-start(), calls=%async_computation.50 | async-start | bytes 1179648
  851.6 905.9 %reduce-scatter.65.cloned.1.call-start = ((), (), s32[]{:S(2)}) async-start(), calls=%async_computation.46 | async-start | bytes 2654208
  950.1 845.2 %reduce-scatter.67.cloned.1.call-start = ((), (), s32[]{:S(2)}) async-start(), calls=%async_computation.47 | async-start | bytes 2654208
  1048.2 784.8 %reduce-scatter.69.cloned.1.call-start = ((), (), s32[]{:S(2)}) async-start(), calls=%async_computation.48 | async-start | bytes 2654208
  1146.4 724.5 %reduce-scatter.71.cloned.1.call-start = ((), (), s32[]{:S(2)}) async-start(), calls=%async_computation.49 | async-start | bytes 2654208
  (236 other events, 3963.7 us)
Sparse Core Ops, SparseCore 0:
  112.1 56.5 all-gather.32
  171.0 57.1 all-gather.36
  230.0 35.1 all-gather.38
  267.0 40.4 all-gather.40
  310.0 57.5 all-gather.44
  369.3 57.0 all-gather.48
  667.4 30.8 reduce-scatter.62
  707.1 30.5 reduce-scatter.60
  740.6 52.6 reduce-scatter.54
  796.3 52.6 reduce-scatter.52
  852.0 94.9 reduce-scatter.44
  950.0 95.0 reduce-scatter.46
  1048.2 95.0 reduce-scatter.48
  1146.2 95.0 reduce-scatter.50
  1273.8 28.2 reduce-scatter.78
  1304.9 29.0 reduce-scatter.42
  1336.8 29.0 reduce-scatter.40
  1372.9 282.9 all-reduce.40
  1658.6 28.5 reduce-scatter.74
  1689.9 30.8 reduce-scatter.72
  1723.1 34.4 reduce-scatter.64
  1759.9 35.4 reduce-scatter.66
  1797.5 35.4 reduce-scatter.68
  1835.4 35.4 reduce-scatter.70
  (7 shorter events, 168.1 us)
where the time goes:
time: 1960 us; the launch traced here: 1940 us
  waiting for transfers between devices  1050 us (54%)
  matrix products  256 us (13%)
  blocking collectives  237 us (12%)
  local copies, waits for them, and re-layouts  188 us (10%)
  other arithmetic  170 us (9%)
  between operations  24.2 us (1%)
  starting transfers between devices  22.2 us (1%)
    reduce_scatter x8, waiting for transfers between devices, reduce_grad(): rows = lax.psum_scatter(full, 'fsdp', scatter_dimension=0, tiled=True)  381 us
    psum x1, waiting for transfers between devices, on_device(): sums_total, counts_total = lax.psum((sums_all, counts_all), ('dp', 'fsdp'))  288 us
    unnamed x41, waiting for transfers between devices  268 us
    all_gather x6, blocking collectives, fetch(): cols = lax.all_gather(shard.astype(jnp.bfloat16), 'dp', axis=1, tiled=True)  106 us
    dot_general x49, matrix products, along_rows(): lax.dot_general(left, right, (((0,), (0,)), ((), ())), preferred_element_...  103 us
    dot_general x41, matrix products, along_cols(): lax.dot_general(left, right, (((1,), (1,)), ((), ())), preferred_element_...  88.1 us
    reduce_scatter x2, waiting for transfers between devices, reduce_grad(): return lax.psum_scatter(rows, 'dp', scatter_dimension=1, tiled=True)  62.3 us
    unnamed x467, local copies, waits for them, and re-layouts  60.6 us
  transfers between devices with their start and end apart: 35, of which 19 were waited for; matrix products, arithmetic and copies ran while one was open for 24% of the time, Pallas kernels for 0%

commit v1 on v0

--- a/solution.py
+++ b/solution.py
@@ -19,6 +19,24 @@
 GAIN_RATE = 0.4
 
 
+def ring_gather(shard, axis, dim):
+    ways, here, step = (lax.axis_size(axis), lax.axis_index(axis), shard.shape[dim])
+    dims = [n * ways if d == dim else n for d, n in enumerate(shard.shape)]
+    full = lax.dynamic_update_slice_in_dim(
+        jnp.zeros(dims, shard.dtype), shard, here * step, axis=dim
+    )
+    going_up = going_down = shard
+    for far in range(1, ways // 2 + 1):
+        going_up = lax.ppermute(going_up, axis, [(d, (d + 1) % ways) for d in range(ways)])
+        full = lax.dynamic_update_slice_in_dim(full, going_up, (here - far) % ways * step, axis=dim)
+        if 2 * far < ways:
+            going_down = lax.ppermute(going_down, axis, [(d, (d - 1) % ways) for d in range(ways)])
+            full = lax.dynamic_update_slice_in_dim(
+                full, going_down, (here + far) % ways * step, axis=dim
+            )
+    return full
+
+
 def geometry(groups, size, width):
     span = jnp.left_shift(jnp.ones_like(groups), groups)
     sides = size // 4 * span
@@ -148,7 +166,7 @@
 
 def fetch(shard):
     cols = lax.all_gather(shard.astype(jnp.bfloat16), "dp", axis=1, tiled=True)
-    return lax.all_gather(cols, "fsdp", axis=0, tiled=True)
+    return ring_gather(cols, "fsdp", 0)
 
 
 def backward_copy(shard, ready):

time: 1960 us -> 2320 us (1.18)
  waiting for transfers between devices: 1050 us -> 1220 us
  local copies, waits for them, and re-layouts: 188 us -> 311 us
  matrix products: 256 us -> 331 us
  blocking collectives: 237 us -> 178 us
  starting transfers between devices: 22.2 us -> 65.3 us
    ppermute x0 -> x30, waiting for transfers between devices: none -> 220 us  [the longest x20 173 us: ring_gather(): lax.ppermute(going_up, axis, [(d, (d + 1) % ways) for d in range(ways)])]
    dynamic_update_slice x0 -> x39, local copies, waits for them, and re-layouts: none -> 72.8 us  [the longest x19 38.7 us: ring_gather(): lax.dynamic_update_slice_in_dim(full, going_up, (here - far) % ways * ste...]
    dot_general x41, matrix products: 88.1 us -> 138 us  [along_cols(): lax.dot_general(left, right, (((1,), (1,)), ((), ())), preferred_element_...]
    all_gather x4 -> x0, blocking collectives: 44.8 us -> none  [fetch(): return lax.all_gather(cols, 'fsdp', axis=0, tiled=True)]
    all_gather x4, waiting for transfers between devices: 44.7 us -> 0.01 us  [fetch(): cols = lax.all_gather(shard.astype(jnp.bfloat16), 'dp', axis=1, tiled=True)]
    ppermute x0 -> x30, starting transfers between devices: none -> 44.6 us  [the longest x20 27.2 us: ring_gather(): lax.ppermute(going_up, axis, [(d, (d + 1) % ways) for d in range(ways)])]
    unnamed x467 -> x505, local copies, waits for them, and re-layouts: 60.6 us -> 58.9 us
    unnamed x41 -> x35, waiting for transfers between devices: 268 us -> 267 us
  transfers between devices with their start and end apart: 35 -> 59, of which waited for: 19 -> 26; matrix products, arithmetic and copies ran while one was open for 24% -> 26% of each run, Pallas kernels for 0% -> 0%
where the time goes in v1:
time: 2320 us; the launch traced here: 2300 us
  waiting for transfers between devices  1220 us (53%)
  matrix products  331 us (14%)
  local copies, waits for them, and re-layouts  311 us (13%)
  blocking collectives  178 us (8%)
  other arithmetic  171 us (7%)
  starting transfers between devices  65.3 us (3%)
  between operations  24.4 us (1%)
    reduce_scatter x8, waiting for transfers between devices, reduce_grad(): rows = lax.psum_scatter(full, 'fsdp', scatter_dimension=0, tiled=True)  386 us
    psum x1, waiting for transfers between devices, on_device(): sums_total, counts_total = lax.psum((sums_all, counts_all), ('dp', 'fsdp'))  288 us
    unnamed x35, waiting for transfers between devices  267 us
    ppermute x20, waiting for transfers between devices, ring_gather(): lax.ppermute(going_up, axis, [(d, (d + 1) % ways) for d in range(ways)])  173 us
    dot_general x41, matrix products, along_cols(): lax.dot_general(left, right, (((1,), (1,)), ((), ())), preferred_element_...  138 us
    dot_general x49, matrix products, along_rows(): lax.dot_general(left, right, (((0,), (0,)), ((), ())), preferred_element_...  103 us
    all_gather x6, blocking collectives, fetch(): cols = lax.all_gather(shard.astype(jnp.bfloat16), 'dp', axis=1, tiled=True)  91.2 us
    dot_general x36, matrix products, conv_forward(): jnp.dot(piece, taps[index], preferred_element_type=jnp.float32)  62.4 us
  transfers between devices with their start and end apart: 59, of which 26 were waited for; matrix products, arithmetic and copies ran while one was open for 26% of the time, Pallas kernels for 0%

profile of v1, /device:TPU:12, one launch (start us, length us, event | category | flops | bytes accessed | tf_op | source)
XLA Modules:
  0.0 2304.5 jit_solution(10111510585663786556)
XLA Ops:
  365.2 44.4 %collective-permute-done.6 = bf16[1152,512]{1,0:T(8,128)(2,1)} collective-permute-done((bf16[1152,512]{1,0:T(8,128)(2,1)}, bf16[1152,512]{1,0:T(8,128)(2,1)}, u32[]{:S(2)}, u32[]{:S(2)}) %collective-permute-start.6) | collective-permute-done | bytes 1179680 | tf_op jit(solution)/shard_map/ppermute | solution.py:30
  417.3 42.8 %collective-permute-done.21 = bf16[1152,512]{1,0:T(8,128)(2,1)} collective-permute-done((bf16[1152,512]{1,0:T(8,128)(2,1)}, bf16[1152,512]{1,0:T(8,128)(2,1)}, u32[]{:S(2)}, u32[]{:S(2)}) %collective-permute-start.21) | collective-permute-done | bytes 1179680 | tf_op jit(solution)/shard_map/ppermute | solution.py:30
  488.3 22.3 collective-permute-done.22
  511.7 24.2 %collective-permute-done.25 = bf16[1152,512]{1,0:T(8,128)(2,1)S(1)} collective-permute-done((bf16[1152,512]{1,0:T(8,128)(2,1)S(1)}, bf16[1152,512]{1,0:T(8,128)(2,1)S(1)}, u32[]{:S(2)}, u32[]{:S(2)}) %collective-permute-start.25) | collective-permute-done | bytes 1179680 | tf_op jit(solution)/shard_map/ppermute | solution.py:33
  537.0 24.2 %collective-permute-done.5 = bf16[1152,512]{1,0:T(8,128)(2,1)S(1)} collective-permute-done((bf16[1152,512]{1,0:T(8,128)(2,1)}, bf16[1152,512]{1,0:T(8,128)(2,1)S(1)}, u32[]{:S(2)}, u32[]{:S(2)}) %collective-permute-start.5) | collective-permute-done | bytes 1179680 | tf_op jit(solution)/shard_map/ppermute | solution.py:30
  561.1 25.3 %collective-permute-done.23 = bf16[1152,512]{1,0:T(8,128)(2,1)S(1)} collective-permute-done((bf16[1152,512]{1,0:T(8,128)(2,1)}, bf16[1152,512]{1,0:T(8,128)(2,1)S(1)}, u32[]{:S(2)}, u32[]{:S(2)}) %collective-permute-start.23) | collective-permute-done | bytes 1179680 | tf_op jit(solution)/shard_map/ppermute | solution.py:30
  774.8 41.6 %psum.50 = f32[]{:T(128)} all-reduce(f32[]{:T(128)} %get-tuple-element.298), channel_id=1, replica_groups=mesh['dp'=8,'fsdp'=4] {'dp','fsdp'}, use_global_device_ids=true, to_apply=%region_27.30 | all-reduce | flops 1 | bytes 8 | tf_op jit(solution)/shard_map/psum | solution.py:235
  1150.2 49.5 %while.36 = (s32[]{:T(128)}, f32[8,2048,256]{2,1,0:T(8,128)}, f32[8,2048]{1,0:T(8,128)S(1)}, s32[4,256]{1,0:T(4,128)S(1)}, s32[8]{0:T(128)S(1)}, /*index=5*/bf16[1024,256]{1,0:T(8,128)(2,1)S(1)}, s32[]{:T(128)}, s32[]{:T(128)}) while((s32[]{:T(128)}, f32[8,2048,256]{2,1,0:T(8,128)}, f32[8,2048]{1,0:T(8,128)S(1)}, s32[4,256]{1,0:T(4,128)S(1)}, ...), condition=%wide.region_84.87_spmd, body=%wide.region_82.86_spmd.sunk | while | flops 1084227584 | bytes 2687093 | solution.py:373
  1211.7 95.5 %reduce-scatter.45.cloned.1.call-done = f32[1152,512]{1,0:T(8,128)} async-done(((f32[4608,512]{1,0:T(8,128)}), f32[1152,512]{1,0:T(8,128)}) %reduce-scatter.45.cloned.1.call-update) | async-done | bytes 2359312 | tf_op jit(solution)/shard_map/reduce_scatter | solution.py:177
  1310.7 94.6 %reduce-scatter.47.cloned.1.call-done = f32[1152,512]{1,0:T(8,128)} async-done(((f32[4608,512]{1,0:T(8,128)}), f32[1152,512]{1,0:T(8,128)}) %reduce-scatter.47.cloned.1.call-update) | async-done | bytes 2359312 | tf_op jit(solution)/shard_map/reduce_scatter | solution.py:177
  1408.4 95.0 %reduce-scatter.49.cloned.1.call-done = f32[1152,512]{1,0:T(8,128)} async-done(((f32[4608,512]{1,0:T(8,128)}), f32[1152,512]{1,0:T(8,128)}) %reduce-scatter.49.cloned.1.call-update) | async-done | bytes 2359312 | tf_op jit(solution)/shard_map/reduce_scatter | solution.py:177
  1506.6 94.9 %reduce-scatter.51.cloned.1.call-done = f32[1152,512]{1,0:T(8,128)} async-done(((f32[4608,512]{1,0:T(8,128)}), f32[1152,512]{1,0:T(8,128)}) %reduce-scatter.51.cloned.1.call-update) | async-done | bytes 2359312 | tf_op jit(solution)/shard_map/reduce_scatter | solution.py:177
  1606.0 24.8 %reduce-scatter.77.cloned.1.call-done = f32[32,128]{1,0:T(8,128)} async-done(((f32[256,128]{1,0:T(8,128)}), f32[32,128]{1,0:T(8,128)}) %reduce-scatter.77.cloned.1.call-update) | async-done | bytes 16400
  1631.7 30.2 %reduce-scatter.79.cloned.1.call-done = f32[32,128]{1,0:T(8,128)} async-done(((f32[256,128]{1,0:T(8,128)}), f32[32,128]{1,0:T(8,128)}) %reduce-scatter.79.cloned.1.call-update) | async-done | bytes 16400
  1663.4 30.3 %reduce-scatter.43.cloned.1.call-done = f32[192,64]{0,1:T(8,128)} async-done(((f32[192,512]{0,1:T(8,128)}), f32[192,64]{0,1:T(8,128)}) %reduce-scatter.43.cloned.1.call-update) | async-done | bytes 49168 | tf_op jit(solution)/shard_map/reduce_scatter | solution.py:178
  1693.7 31.9 %reduce-scatter.41.cloned.1.call-done = f32[192,64]{0,1:T(8,128)} async-done(((f32[192,512]{0,1:T(8,128)}), f32[192,64]{0,1:T(8,128)}) %reduce-scatter.41.cloned.1.call-update) | async-done | bytes 49168 | tf_op jit(solution)/shard_map/reduce_scatter | solution.py:178
  1727.1 288.4 %all-reduce.41.cloned.1.call-done = (f32[16384]{0:T(1024)}, f32[16384,256]{1,0:T(8,128)}) async-done(((f32[16384]{0:T(1024)}, f32[16384,256]{1,0:T(8,128)}), (f32[16384]{0:T(1024)}, f32[16384,256]{1,0:T(8,128)})) %all-reduce.41.cloned.1.call-update) | async-done | bytes 16842768 | tf_op jit(solution)/shard_map/psum | solution.py:376
  2018.5 28.5 %reduce-scatter.75.cloned.1.call-done = f32[64,512]{1,0:T(8,128)} async-done(((f32[512,512]{1,0:T(8,128)}), f32[64,512]{1,0:T(8,128)}) %reduce-scatter.75.cloned.1.call-update) | async-done | bytes 131088
  2047.0 33.5 %reduce-scatter.73.cloned.1.call-done = f32[64,512]{1,0:T(8,128)} async-done(((f32[512,512]{1,0:T(8,128)}), f32[64,512]{1,0:T(8,128)}) %reduce-scatter.73.cloned.1.call-update) | async-done | bytes 131088
  2082.2 35.2 %reduce-scatter.65.cloned.1.call-done = f32[64,1152]{1,0:T(8,128)} async-done(((f32[512,1152]{1,0:T(8,128)}), f32[64,1152]{1,0:T(8,128)}) %reduce-scatter.65.cloned.1.call-update) | async-done | bytes 294928
  2117.4 37.8 %reduce-scatter.67.cloned.1.call-done = f32[64,1152]{1,0:T(8,128)} async-done(((f32[512,1152]{1,0:T(8,128)}), f32[64,1152]{1,0:T(8,128)}) %reduce-scatter.67.cloned.1.call-update) | async-done | bytes 294928
  2155.2 37.6 %reduce-scatter.69.cloned.1.call-done = f32[64,1152]{1,0:T(8,128)} async-done(((f32[512,1152]{1,0:T(8,128)}), f32[64,1152]{1,0:T(8,128)}) %reduce-scatter.69.cloned.1.call-update) | async-done | bytes 294928
  2192.9 37.8 %reduce-scatter.71.cloned.1.call-done = f32[64,1152]{1,0:T(8,128)} async-done(((f32[512,1152]{1,0:T(8,128)}), f32[64,1152]{1,0:T(8,128)}) %reduce-scatter.71.cloned.1.call-update) | async-done | bytes 294928
  2235.6 44.7 %all-reduce.37 = (f32[1]{0:T(128)}, f32[1]{0:T(128)}, f32[]{:T(128)}, f32[8,512]{1,0:T(8,128)}) all-reduce(f32[1]{0:T(128)} %bitcast.148, f32[1]{0:T(128)} %bitcast.146, f32[]{:T(128)S(6)} %add.1566, f32[8,512]{1,0:T(8,128)} %stack.107), channel_id=1, replica_groups=mesh['dp'=8,'fsdp'=4] {'dp','fsdp'}, use_global_device_ids=true, to_apply=%region_29.32 | all-reduce | flops 4099 | bytes 32792 | tf_op jit(solution)/shard_map/psum | solution.py:340
  (1197 shorter events, 1022.0 us)
Async XLA Ops:
  7.2 311.8 %all-gather.15.cloned.1.call-start = ((), (), s32[]{:S(2)}) async-start(), calls=%async_computation.34 | async-start | bytes 1327104 | tf_op jit(solution)/shard_map/all_gather | solution.py:168
  9.5 314.9 %all-gather.17.cloned.1.call-start = ((), (), s32[]{:S(2)}) async-start(), calls=%async_computation.35 | async-start | bytes 1327104 | tf_op jit(solution)/shard_map/all_gather | solution.py:168
  10.2 319.4 %all-gather.19.cloned.1.call-start = ((), (), s32[]{:S(2)}) async-start(), calls=%async_computation.36 | async-start | bytes 1327104 | tf_op jit(solution)/shard_map/all_gather | solution.py:168
  24.5 176.3 %collective-permute-start.12 = (bf16[128,256]{0,1:T(8,128)(2,1)S(1)}, bf16[128,256]{0,1:T(8,128)(2,1)}, u32[]{:S(2)}, u32[]{:S(2)}) collective-permute-start(bf16[128,256]{0,1:T(8,128)(2,1)S(1)} %bitcast.1048), channel_id=1, source_target_pairs={{0,1},{1,2},{2,3},{3,0},{4,5},{5,6},{6,7},{7,4},{8,9},{9,10},{10,1... | collective-permute-start | bytes 196616 | tf_op jit(solution)/shard_map/ppermute | solution.py:30
  26.0 179.6 %collective-permute-start.13 = (bf16[128,256]{0,1:T(8,128)(2,1)S(1)}, bf16[128,256]{0,1:T(8,128)(2,1)}, u32[]{:S(2)}, u32[]{:S(2)}) collective-permute-start(bf16[128,256]{0,1:T(8,128)(2,1)S(1)} %bitcast.1049), channel_id=1, source_target_pairs={{0,3},{1,0},{2,1},{3,2},{4,7},{5,4},{6,5},{7,6},{8,11},{9,8},{10,9... | collective-permute-start | bytes 196616 | tf_op jit(solution)/shard_map/ppermute | solution.py:33
  98.5 257.3 %all-gather.21.cloned.1.call-start = ((), (), s32[]{:S(2)}) async-start(), calls=%async_computation.37 | async-start | bytes 1327104 | tf_op jit(solution)/shard_map/all_gather | solution.py:168
  319.1 823.3 %reduce-scatter.57.cloned.1.call-start = ((), (), s32[]{:S(2)}) async-start(), calls=%async_computation.32 | async-start | bytes 655360 | tf_op jit(solution)/shard_map/reduce_scatter | solution.py:177
  510.6 238.6 %collective-permute-start.26 = (bf16[1152,512]{1,0:T(8,128)(2,1)}, bf16[1152,512]{1,0:T(8,128)(2,1)}, u32[]{:S(2)}, u32[]{:S(2)}) collective-permute-start(bf16[1152,512]{1,0:T(8,128)(2,1)} %collective-permute-done.24), channel_id=1, source_target_pairs={{0,1},{1,2},{2,3},{3,0},{4,5},{5,6},{6,7},{7,4},{8,9},{9,10},{10,1... | collective-permute-start | bytes 3538952 | tf_op jit(solution)/shard_map/ppermute | solution.py:30
  962.7 181.5 %reduce-scatter.59.cloned.1.call-start = ((), (), s32[]{:S(2)}) async-start(), calls=%async_computation.33 | async-start | bytes 655360 | tf_op jit(solution)/shard_map/reduce_scatter | solution.py:177
  1069.2 238.1 %reduce-scatter.45.cloned.1.call-start = ((), (), s32[]{:S(2)}) async-start(), calls=%async_computation.26 | async-start | bytes 11796480 | tf_op jit(solution)/shard_map/reduce_scatter | solution.py:177
  1085.8 319.4 %reduce-scatter.47.cloned.1.call-start = ((), (), s32[]{:S(2)}) async-start(), calls=%async_computation.27 | async-start | bytes 11796480 | tf_op jit(solution)/shard_map/reduce_scatter | solution.py:177
  1103.1 400.4 %reduce-scatter.49.cloned.1.call-start = ((), (), s32[]{:S(2)}) async-start(), calls=%async_computation.28 | async-start | bytes 11796480 | tf_op jit(solution)/shard_map/reduce_scatter | solution.py:177
  1125.0 476.5 %reduce-scatter.51.cloned.1.call-start = ((), (), s32[]{:S(2)}) async-start(), calls=%async_computation.29 | async-start | bytes 11796480 | tf_op jit(solution)/shard_map/reduce_scatter | solution.py:177
  1142.3 488.5 %reduce-scatter.77.cloned.1.call-start = ((), (), s32[]{:S(2)}) async-start(), calls=%async_computation.46 | async-start | bytes 147456
  1144.1 517.8 %reduce-scatter.79.cloned.1.call-start = ((), (), s32[]{:S(2)}) async-start(), calls=%async_computation.47 | async-start | bytes 147456
  1145.9 547.8 %reduce-scatter.43.cloned.1.call-start = ((), (), s32[]{:S(2)}) async-start(), calls=%async_computation.25 | async-start | bytes 589824 | tf_op jit(solution)/shard_map/reduce_scatter | solution.py:178
  1148.0 577.6 %reduce-scatter.41.cloned.1.call-start = ((), (), s32[]{:S(2)}) async-start(), calls=%async_computation.24 | async-start | bytes 589824 | tf_op jit(solution)/shard_map/reduce_scatter | solution.py:178
  1150.1 865.4 %all-reduce.41.cloned.1.call-start = ((), (), s32[]{:S(2)}) async-start(), calls=%async_computation.48 | async-start | bytes 33685504 | tf_op jit(solution)/shard_map/psum | solution.py:376
  1200.4 846.6 %reduce-scatter.75.cloned.1.call-start = ((), (), s32[]{:S(2)}) async-start(), calls=%async_computation.45 | async-start | bytes 1179648
  1203.0 877.5 %reduce-scatter.73.cloned.1.call-start = ((), (), s32[]{:S(2)}) async-start(), calls=%async_computation.44 | async-start | bytes 1179648
  1211.7 905.8 %reduce-scatter.65.cloned.1.call-start = ((), (), s32[]{:S(2)}) async-start(), calls=%async_computation.40 | async-start | bytes 2654208
  1310.4 844.9 %reduce-scatter.67.cloned.1.call-start = ((), (), s32[]{:S(2)}) async-start(), calls=%async_computation.41 | async-start | bytes 2654208
  1408.4 784.5 %reduce-scatter.69.cloned.1.call-start = ((), (), s32[]{:S(2)}) async-start(), calls=%async_computation.42 | async-start | bytes 2654208
  1506.6 724.1 %reduce-scatter.71.cloned.1.call-start = ((), (), s32[]{:S(2)}) async-start(), calls=%async_computation.43 | async-start | bytes 2654208
  (279 other events, 6532.6 us)
Sparse Core Ops, SparseCore 0:
  10.3 23.7 all-gather.14
  61.0 23.1 all-gather.18
  113.9 25.9 all-gather.20
  962.9 23.7 reduce-scatter.56
  1005.9 23.8 reduce-scatter.58
  1032.8 30.8 reduce-scatter.62
  1066.7 30.9 reduce-scatter.60
  1100.6 52.6 reduce-scatter.54
  1156.4 52.6 reduce-scatter.52
  1212.2 94.9 reduce-scatter.44
  1310.2 95.0 reduce-scatter.46
  1408.4 95.0 reduce-scatter.48
  1506.4 95.0 reduce-scatter.50
  1604.2 26.6 reduce-scatter.76
  1633.6 28.2 reduce-scatter.78
  1664.6 29.0 reduce-scatter.42
  1696.5 29.1 reduce-scatter.40
  1732.6 282.8 all-reduce.40
  2018.3 28.7 reduce-scatter.74
  2049.9 30.6 reduce-scatter.72
  2082.9 34.4 reduce-scatter.64
  2119.8 35.4 reduce-scatter.66
  2157.4 35.4 reduce-scatter.68
  2195.2 35.4 reduce-scatter.70
  (1 shorter events, 22.4 us)
